TPU v7x, 512 devices: a whole 4x8x8 slice. The times are simulated.
512 devices in a mesh: dp: 4 (over z_lo, core), ctx: 32 (over z_hi, y), tp: 4 (over x).
Axes of the slice: x: 4, y: 8, z: 8 (z_hi: 4, z_lo: 2; z = z_hi * 2 + z_lo), core: 2. Of those that a mesh axis runs over, the one named last changes fastest.
Arguments:
- queries: bfloat16 [16384, 4096], P(('dp', 'ctx'), 'tp'), parts along dimension 0, may hold values from -40 to 40
- keys: bfloat16 [16384, 4096], P(('dp', 'ctx'), 'tp'), parts along dimension 0, may hold values from -40 to 40
- values: bfloat16 [16384, 4096], P(('dp', 'ctx'), 'tp'), parts along dimension 0, may hold values from -6 to 6
- query_gain: float32 [4096], P('tp'), may hold values from 0.1 to 1.9
- key_gain: float32 [4096], P('tp'), may hold values from 0.1 to 1.9
- block_mask: int32 [32, 32], P('ctx'), may hold values from 0 to 1, as said below
Outputs:
- attended: bfloat16 [16384, 4096], P(('dp', 'ctx'), 'tp'), parts along dimension 0
There are 4 independent parts, one for each index of `dp`. A program takes and returns all parts, laid end to end along the dimension named above; an argument that names none is the same for every part. Nothing has to cross between parts.
Inputs may be any that keep to these rules, and one draw needn't show every extreme that they name: block_mask[i, i] is 1 for every i, and block_mask[i, j] is 0 unless |i - j| is a power of two.
All inputs are finite; a program needn't handle non-finite values.
Results may differ from a plain program's by a relative error of at most 0.011.
Values may be sent and summed in bfloat16 or wider, within the bound.
No kernel may reach another device: no remote copies, remote signals or barrier semaphores. Data moves between devices by JAX's collectives and lax.ppermute only.
A program may use at most 128 MiB of HBM per device.

v0:
```python
import jax
import jax.numpy as jnp
from jax import lax
from jax.sharding import PartitionSpec as P

HEADS = 32
HD = 128
BLOCK = 128


epsilon = 1e-06
floor_score = -1e30


def normalize(raw_rows, total_sq, gain_vec, full_width):
    as_float = raw_rows.astype(jnp.float32)
    factor = lax.rsqrt(total_sq / full_width + epsilon)
    return (as_float * factor[:, None] * gain_vec[None, :]).astype(jnp.bfloat16)


def expand_mask(mask_part, block_len):
    q_blocks, k_blocks = mask_part.shape
    spread_out = jnp.broadcast_to(
        mask_part[:, None, :, None], (q_blocks, block_len, k_blocks, block_len)
    )
    return spread_out.reshape(q_blocks * block_len, k_blocks * block_len) > 0


def local(queries, keys, values, query_gain, key_gain, block_mask):
    tok_rows, row_width = queries.shape
    head_count = row_width // HD
    sq_queries = jnp.sum(jnp.square(queries.astype(jnp.float32)), axis=1)
    sq_keys = jnp.sum(jnp.square(keys.astype(jnp.float32)), axis=1)
    tot_queries, tot_keys = lax.psum((sq_queries, sq_keys), "tp")
    full_width = HEADS * HD
    q_normed = normalize(queries, tot_queries, query_gain, full_width).reshape(
        tok_rows, head_count, HD
    )
    k_normed = normalize(keys, tot_keys, key_gain, full_width).reshape(tok_rows, head_count, HD)
    v_heads = values.reshape(tok_rows, head_count, HD)
    score_scale = HD ** (-0.5)
    key_piece = lax.all_gather(k_normed, "ctx", axis=0, tiled=True)
    value_piece = lax.all_gather(v_heads, "ctx", axis=0, tiled=True)
    run_max = jnp.full((head_count, tok_rows), floor_score, jnp.float32)
    run_acc = jnp.zeros((tok_rows, head_count, HD), jnp.float32)
    allowed = expand_mask(block_mask, BLOCK)[None]
    scores = (
        jnp.einsum("qhd,khd->hqk", q_normed, key_piece, preferred_element_type=jnp.float32)
        * score_scale
    )
    scores = jnp.where(allowed, scores, floor_score)
    new_max = jnp.maximum(run_max, jnp.max(scores, axis=2))
    shrink = jnp.exp(run_max - new_max)
    weights = jnp.where(allowed, jnp.exp(scores - new_max[:, :, None]), 0.0)
    new_sum = jnp.sum(weights, axis=2)
    update = jnp.einsum(
        "hqk,khd->qhd",
        weights.astype(jnp.bfloat16),
        value_piece,
        preferred_element_type=jnp.float32,
    )
    new_acc = run_acc * shrink.T[:, :, None] + update
    result = new_acc / new_sum.T[:, :, None]
    return result.astype(jnp.bfloat16).reshape(tok_rows, row_width)


def solution(mesh):
    in_specs = (
        P(("dp", "ctx"), "tp"),
        P(("dp", "ctx"), "tp"),
        P(("dp", "ctx"), "tp"),
        P("tp"),
        P("tp"),
        P("ctx", None),
    )
    out_specs = P(("dp", "ctx"), "tp")
    return jax.shard_map(local, mesh=mesh, in_specs=in_specs, out_specs=out_specs, check_vma=False)
```

profile of v0, /device:TPU:6, one launch (start us, length us, event | category | flops | bytes accessed | tf_op | source)
XLA Modules:
  0.0 330.5 jit_solution(13819743713990285720)
XLA Ops:
  6.5 0.0 all-gather.3.cloned.1.call-start
  6.5 1.1 copy.10
  7.7 0.2 fusion.21
  7.8 1.1 fusion.18
  8.9 12.3 %all-reduce = (f32[128]{0:T(128)S(1)}, f32[128]{0:T(128)S(1)}) all-reduce(f32[128]{0:T(128)S(1)} %fusion.21, f32[128]{0:T(128)S(1)} %fusion.18), channel_id=1, replica_groups=mesh['dp'=4,'ctx'=32,'tp'=4] {'tp'}, use_global_device_ids=true, to_apply=%region_3.0 | all-reduce | flops 256 | bytes 2048 | tf_op jit(solution)/shard_map/psum | solution.py:34
  21.2 0.9 fusion.23
  22.1 0.8 copy.11
  23.0 0.0 all-gather.3.cloned.1.call-update
  23.0 0.0 all-gather.5.cloned.1.call-start
  23.1 1.8 copy.13
  24.8 0.0 all-gather.5.cloned.1.call-update
  24.9 0.7 compare_bitcast_fusion
  25.5 0.1 broadcast_bitcast_fusion
  25.6 138.3 %all-gather.3.cloned.1.call-done = bf16[4096,8,128]{2,0,1:T(8,128)(2,1)} async-done(((bf16[128,8,128]{2,0,1:T(8,128)(2,1)}), bf16[4096,8,128]{2,0,1:T(8,128)(2,1)}) %all-gather.3.cloned.1.call-update) | async-done | bytes 8388624 | tf_op jit(solution)/shard_map/all_gather | solution.py:42
  163.9 11.7 %fusion = (f32[8,128]{1,0:T(8,128)S(1)}, f32[8,128,4096]{2,1,0:T(8,128)}) fusion(pred[4096]{0:T(1024)(128)(4,1)S(1)} %broadcast_bitcast_fusion, bf16[4096,8,128]{2,0,1:T(8,128)(2,1)} %all-gather.3.cloned.1.call-done, bf16[128,1024]{1,0:T(8,128)(2,1)} %param.6, f32[1024]{0:T(1024)} %param.9, f32[128]{0:T(128)S(1)} %add_rsqrt_fusion.1), kind=kOutput, calls=%fused_computation.2 | convolution fusion | flops 1086848000 | bytes 25440768 | tf_op jit(solution)/shard_map/qhd,khd->hqk/dot_general | solution.py:48
  175.6 8.5 %fusion.1 = f32[8,128]{1,0:T(8,128)S(1)} fusion(f32[8,128,4096]{2,1,0:T(8,128)} %get-tuple-element.10, f32[8,128]{1,0:T(8,128)S(1)} %get-tuple-element.8, pred[4096]{0:T(1024)(128)(4,1)S(1)} %broadcast_bitcast_fusion), kind=kLoop, calls=%fused_computation.3 | loop fusion | flops 20970496 | bytes 16789504 | tf_op jit(solution)/shard_map/reduce_sum | solution.py:55
  184.1 128.0 %all-gather.5.cloned.1.call-done = bf16[4096,8,128]{0,2,1:T(8,128)(2,1)} async-done(((bf16[128,8,128]{0,2,1:T(8,128)(2,1)}), bf16[4096,8,128]{0,2,1:T(8,128)(2,1)}) %all-gather.5.cloned.1.call-update) | async-done | bytes 8388624 | tf_op jit(solution)/shard_map/all_gather | solution.py:43
  312.2 10.6 %fusion.15 = bf16[128,8,128]{0,2,1:T(8,128)(2,1)S(1)} fusion(bf16[4096,8,128]{0,2,1:T(8,128)(2,1)} %all-gather.5.cloned.1.call-done, f32[8,128,4096]{2,1,0:T(8,128)} %get-tuple-element.10, f32[8,128]{1,0:T(8,128)S(1)} %get-tuple-element.8, pred[4096]{0:T(1024)(128)(4,1)S(1)} %broadcast_bitcast_fusion, f32[128,8]{0,1:T(8,128)S(1)} %bitcast.32, ...), kind=kOutput, calls=%fused_computation.10 | convolution fusion | flops 1095106560 | bytes 25444352 | tf_op jit(solution)/shard_map/hqk,khd->qhd/dot_general | solution.py:56
  322.8 0.8 copy.14
  (3 shorter events, 0.0 us)
Async XLA Ops:
  6.5 157.4 %all-gather.3.cloned.1.call-start = ((), (), s32[]{:S(2)}) async-start(), calls=%async_computation | async-start | bytes 8650752 | tf_op jit(solution)/shard_map/all_gather | solution.py:42
  23.0 289.2 %all-gather.5.cloned.1.call-start = ((), (), s32[]{:S(2)}) async-start(), calls=%async_computation.1 | async-start | bytes 8650752 | tf_op jit(solution)/shard_map/all_gather | solution.py:43
Sparse Core Ops, SparseCore 0:
  23.1 140.7 all-gather.2
  167.0 145.1 all-gather.4
where the time goes:
time: 331 us
  waiting for transfers between devices  266 us (80%)
  matrix products  22.3 us (7%)
  between operations  13.4 us (4%)
  blocking collectives  12.3 us (4%)
  other arithmetic  11.3 us (3%)
  local copies, waits for them, and re-layouts  4.67 us (1%)
    all_gather x1, waiting for transfers between devices, local(): key_piece = lax.all_gather(k_normed, 'ctx', axis=0, tiled=True)  138 us
    all_gather x1, waiting for transfers between devices, local(): value_piece = lax.all_gather(v_heads, 'ctx', axis=0, tiled=True)  128 us
    psum x1, blocking collectives, local(): tot_queries, tot_keys = lax.psum((sq_queries, sq_keys), 'tp')  12.3 us
    dot_general x1, matrix products, local(): jnp.einsum('qhd,khd->hqk', q_normed, key_piece, preferred_element_type=jn...  11.7 us
    dot_general x1, matrix products, local(): jnp.einsum('hqk,khd->qhd', weights.astype(jnp.bfloat16), value_piece, pre...  10.6 us
    reduce_sum x1, other arithmetic, local(): new_sum = jnp.sum(weights, axis=2)  8.51 us
  transfers between devices with their start and end apart: 2, of which 2 were waited for; matrix products, arithmetic and copies ran while one was open for 7% of the time, Pallas kernels for 0%

commit v1 on v0

v1 whole, which is shorter than its diff:
```python
import jax
import jax.numpy as jnp
from jax import lax
from jax.experimental import pallas as pl
from jax.experimental.pallas import tpu as pltpu
from jax.sharding import PartitionSpec as P

HEADS = 32
HD = 128
BLOCK = 128
ROW = 8
EXTRA = 16

epsilon = 1e-06
floor_score = -1e30
OFFSETS = (0, 1, -1, 2, -2, 4, -4, 8, -8)


def prep_kernel(q_ref, k_ref, v_ref, tot_ref, qg_ref, kg_ref, mask_ref, kv_ref, qm_ref):
    factor = lax.rsqrt(tot_ref[...] / (HEADS * HD) + epsilon)
    columns = jnp.transpose(factor)
    qf, kf = columns[:, 0:1], columns[:, 1:2]
    row = jnp.broadcast_to(mask_ref[...], (EXTRA, BLOCK)).astype(jnp.bfloat16)
    for h in range(ROW):
        cut = slice(h * HD, (h + 1) * HD)
        k = k_ref[:, cut].astype(jnp.float32) * kf * kg_ref[:, cut]
        kv_ref[h, :BLOCK, :] = k.astype(jnp.bfloat16)
        kv_ref[h, BLOCK:, :] = v_ref[:, cut]
        q = q_ref[:, cut].astype(jnp.float32) * qf * qg_ref[:, cut]
        qm_ref[h, :BLOCK, :] = q.astype(jnp.bfloat16)
        qm_ref[h, BLOCK:, :] = row


def attend_kernel(flag_ref, qm_ref, own_ref, prev_ref, next_ref, opp_ref, out_ref):
    rows = (prev_ref, own_ref, next_ref)
    for i in range(ROW):
        blocks = []
        for d in OFFSETS:
            j = ROW + i + d
            blocks.append((rows[j // ROW], j % ROW))
        blocks.append((opp_ref, i))
        q = qm_ref[i, :BLOCK, :]
        keys = jnp.concatenate([r[j, :BLOCK, :] for r, j in blocks], axis=0)
        scores = lax.dot_general(
            q, keys, (((1,), (1,)), ((), ())), preferred_element_type=jnp.float32
        ) * (HD ** (-0.5))
        parts = [
            jnp.where(flag_ref[i, n] > 0, scores[:, n * BLOCK : (n + 1) * BLOCK], floor_score)
            for n in range(len(blocks))
        ]
        top = parts[0]
        for part in parts[1:]:
            top = jnp.maximum(top, part)
        row_max = jnp.max(top, axis=1, keepdims=True)
        weights = [jnp.exp(part - row_max) for part in parts]
        total = weights[0]
        for w in weights[1:]:
            total = total + w
        weight_sum = jnp.sum(total, axis=1, keepdims=True)
        rounded = jnp.concatenate([w.astype(jnp.bfloat16) for w in weights], axis=1)
        vals = jnp.concatenate([r[j, BLOCK:, :] for r, j in blocks], axis=0)
        numer = jnp.dot(rounded, vals, preferred_element_type=jnp.float32)
        out_ref[i] = (numer / weight_sum).astype(jnp.bfloat16)


def local(queries, keys, values, query_gain, key_gain, block_mask):
    blocks = block_mask.shape[1]
    rows = blocks // ROW
    groups = [[z * ROW + y for y in range(ROW)] for z in range(rows)]
    z = lax.axis_index("ctx") // ROW

    sums = jnp.stack(
        [jnp.sum(jnp.square(a.astype(jnp.float32)), axis=1) for a in (queries, keys)]
    )
    totals = lax.psum(sums, "tp")
    totals = jnp.pad(totals, ((0, 6), (0, 0)))
    mask_row = jnp.pad(block_mask.astype(jnp.float32), ((0, 0), (0, BLOCK - blocks)))
    kv, qm = pl.pallas_call(
        prep_kernel,
        out_shape=(
            jax.ShapeDtypeStruct((ROW, 2 * BLOCK, HD), jnp.bfloat16),
            jax.ShapeDtypeStruct((ROW, BLOCK + EXTRA, HD), jnp.bfloat16),
        ),
        name="prep",
    )(queries, keys, values, totals, query_gain[None], key_gain[None], mask_row)

    kv = lax.all_to_all(kv, "ctx", 0, 0, axis_index_groups=groups)
    ids = range(blocks)
    ahead = [(c, c + ROW) for c in ids if c + ROW < blocks]
    back = [(c, c - ROW) for c in ids if c >= ROW]
    across = [(c, c ^ 16) for c in ids]
    kv_prev = lax.ppermute(kv, "ctx", ahead)
    kv_next = lax.ppermute(kv, "ctx", back)
    kv_opp = lax.ppermute(kv, "ctx", across)
    qm = lax.all_to_all(qm, "ctx", 0, 0, axis_index_groups=groups)

    centre = z * ROW + jnp.arange(ROW)
    wanted = jnp.stack([centre + d for d in OFFSETS] + [centre ^ 16], axis=1)
    mask_rows = qm[:, BLOCK, :blocks].astype(jnp.float32)
    picked = wanted[:, :, None] == jnp.arange(blocks)[None, None, :]
    flags = jnp.sum(jnp.where(picked, mask_rows[:, None, :], 0.0), axis=2).astype(jnp.int32)

    out = pl.pallas_call(
        attend_kernel,
        out_shape=jax.ShapeDtypeStruct((ROW, BLOCK, HD), jnp.bfloat16),
        in_specs=[pl.BlockSpec(memory_space=pltpu.SMEM)]
        + [pl.BlockSpec(memory_space=pltpu.VMEM)] * 5,
        name="attend",
    )(flags, qm, kv, kv_prev, kv_next, kv_opp)
    out = lax.all_to_all(out, "ctx", 0, 0, axis_index_groups=groups)
    return jnp.transpose(out, (1, 0, 2)).reshape(queries.shape)


def solution(mesh):
    in_specs = (
        P(("dp", "ctx"), "tp"),
        P(("dp", "ctx"), "tp"),
        P(("dp", "ctx"), "tp"),
        P("tp"),
        P("tp"),
        P("ctx", None),
    )
    out_specs = P(("dp", "ctx"), "tp")
    return jax.shard_map(local, mesh=mesh, in_specs=in_specs, out_specs=out_specs, check_vma=False)
```

time: 331 us -> 123 us (0.37)
  waiting for transfers between devices: 266 us -> 50.6 us
  starting transfers between devices: 0.04 us -> 24.6 us
  matrix products: 22.3 us -> 0 us
  blocking collectives: 12.3 us -> 31.2 us
  between operations: 13.4 us -> 0.14 us
  other arithmetic: 11.3 us -> 2.71 us
  Pallas kernels: 0 us -> 7.91 us
    all_gather x2 -> x0, waiting for transfers between devices: 266 us -> none  [the longest x1 138 us: local(): key_piece = lax.all_gather(k_normed, 'ctx', axis=0, tiled=True)]
    ppermute x0 -> x3, waiting for transfers between devices: none -> 36.1 us  [the longest x1 20.3 us: local(): kv_next = lax.ppermute(kv, 'ctx', back)]
    dot_general x2 -> x0, matrix products: 22.3 us -> none  [the longest x1 11.7 us: local(): jnp.einsum('qhd,khd->hqk', q_normed, key_piece, preferred_element_type=jn...]
    all_to_all x0 -> x1, blocking collectives: none -> 18.9 us  [local(): out = lax.all_to_all(out, 'ctx', 0, 0, axis_index_groups=groups)]
    ppermute x0 -> x3, starting transfers between devices: none -> 17.7 us  [the longest x1 10.9 us: local(): kv_opp = lax.ppermute(kv, 'ctx', across)]
    all_to_all x0 -> x2, waiting for transfers between devices: none -> 14.5 us  [the longest x1 14.5 us: local(): kv = lax.all_to_all(kv, 'ctx', 0, 0, axis_index_groups=groups)]
    reduce_sum x3, other arithmetic: 9.75 us -> 1.37 us  [the longest x2 1.22 us: local(): jnp.sum(jnp.square(a.astype(jnp.float32)), axis=1)]
    pallas_call x0 -> x2, Pallas kernels: none -> 7.91 us  [the longest x1 5.6 us: local(): pl.pallas_call(attend_kernel, out_shape=jax.ShapeDtypeStruct((ROW, BLOCK,...]
  transfers between devices with their start and end apart: 2 -> 5, of which waited for: 2 -> 3; matrix products, arithmetic and copies ran while one was open for 7% -> 1% of each run, Pallas kernels for 0% -> 0%
where the time goes in v1:
time: 123 us; the launch traced here: 121 us
  waiting for transfers between devices  50.6 us (41%)
  blocking collectives  31.2 us (25%)
  starting transfers between devices  24.6 us (20%)
  Pallas kernels  7.91 us (6%)
  local copies, waits for them, and re-layouts  3.92 us (3%)
  other arithmetic  2.71 us (2%)
    ppermute x1, waiting for transfers between devices, local(): kv_next = lax.ppermute(kv, 'ctx', back)  20.3 us
    all_to_all x1, blocking collectives, local(): out = lax.all_to_all(out, 'ctx', 0, 0, axis_index_groups=groups)  18.9 us
    ppermute x1, waiting for transfers between devices, local(): kv_opp = lax.ppermute(kv, 'ctx', across)  15.8 us
    all_to_all x1, waiting for transfers between devices, local(): kv = lax.all_to_all(kv, 'ctx', 0, 0, axis_index_groups=groups)  14.5 us
    psum x1, blocking collectives, local(): totals = lax.psum(sums, 'tp')  12.3 us
    ppermute x1, starting transfers between devices, local(): kv_opp = lax.ppermute(kv, 'ctx', across)  10.9 us
    pallas_call x1, Pallas kernels, local(): pl.pallas_call(attend_kernel, out_shape=jax.ShapeDtypeStruct((ROW, BLOCK,...  5.6 us
    ppermute x1, starting transfers between devices, local(): kv_prev = lax.ppermute(kv, 'ctx', ahead)  5.48 us
  transfers between devices with their start and end apart: 5, of which 3 were waited for; matrix products, arithmetic and copies ran while one was open for 1% of the time, Pallas kernels for 0%

profile of v1, /device:TPU:6, one launch (start us, length us, event | category | flops | bytes accessed | tf_op | source)
XLA Modules:
  0.0 121.1 jit_solution(2795377426360440905)
XLA Ops:
  0.0 0.7 convert_element_type.20
  0.7 1.1 multiply_reduce_fusion.1
  1.8 0.1 multiply_reduce_fusion
  1.9 12.3 %psum.7 = f32[2,128]{1,0:T(2,128)S(1)} all-reduce(f32[2,128]{1,0:T(2,128)S(1)} %pad_maximum_fusion), channel_id=1, replica_groups=mesh['dp'=4,'ctx'=32,'tp'=4] {'tp'}, use_global_device_ids=true, to_apply=%region_2.3 | all-reduce | flops 256 | bytes 2048 | tf_op jit(solution)/shard_map/psum | solution.py:75
  14.3 0.6 pad.9.mask_ref
  14.9 0.6 pad.8.tot_ref
  15.4 2.3 %prep.1 = (bf16[8,256,128]{2,1,0:T(8,128)(2,1)}, bf16[8,144,128]{2,1,0:T(8,128)(2,1)}) custom-call(bf16[128,1024]{1,0:T(8,128)(2,1)} %q_ref.1, bf16[128,1024]{1,0:T(8,128)(2,1)} %k_ref.1, bf16[128,1024]{1,0:T(8,128)(2,1)} %v_ref.1, f32[8,128]{1,0:T(8,128)} %pad.8.tot_ref, f32[1,1024]{1,0:T(1,128)} %bitcast.10, f32[1,1024]{1,0:T(1,128)} %bitcast.11, ...), custom_call_target="tpu_custom_call" | custom-call | tf_op jit(solution)/shard_map/prep/pallas_call | solution.py:78
  17.8 3.5 %all-to-all-start.1 = ((bf16[8,256,128]{2,1,0:T(8,128)(2,1)}), bf16[8,256,128]{2,1,0:T(8,128)(2,1)S(1)}, u32[]{:S(2)}, u32[]{:S(2)}) async-start(bf16[8,256,128]{2,1,0:T(8,128)(2,1)} %get-tuple-element.8), calls=%async_computation.1 | async-start | bytes 1048576 | tf_op jit(solution)/shard_map/all_to_all | solution.py:87
  21.3 14.5 %all-to-all-done.1.own_ref = bf16[8,256,128]{2,1,0:T(8,128)(2,1)S(1)} async-done(((bf16[8,256,128]{2,1,0:T(8,128)(2,1)}), bf16[8,256,128]{2,1,0:T(8,128)(2,1)S(1)}, u32[]{:S(2)}, u32[]{:S(2)}) %all-to-all-start.1) | async-done | bytes 524320 | tf_op jit(solution)/shard_map/all_to_all | solution.py:87
  35.8 3.4 %all-to-all-start = ((bf16[8,144,128]{2,1,0:T(8,128)(2,1)}), bf16[8,144,128]{2,1,0:T(8,128)(2,1)S(1)}, u32[]{:S(2)}, u32[]{:S(2)}) async-start(bf16[8,144,128]{2,1,0:T(8,128)(2,1)} %get-tuple-element.7), calls=%async_computation | async-start | bytes 589824 | tf_op jit(solution)/shard_map/all_to_all | solution.py:95
  39.2 10.9 %collective-permute-start.2 = (bf16[8,256,128]{2,1,0:T(8,128)(2,1)S(1)}, bf16[8,256,128]{2,1,0:T(8,128)(2,1)S(1)}, u32[]{:S(2)}, u32[]{:S(2)}) collective-permute-start(bf16[8,256,128]{2,1,0:T(8,128)(2,1)S(1)} %all-to-all-done.1.own_ref), channel_id=1, source_target_pairs={{0,64},{4,68},{8,72},{12,76},{16,80},{20,84},{24,88},{28,92},{32,9... | collective-permute-start | bytes 1572872 | tf_op jit(solution)/shard_map/ppermute | solution.py:94
  50.2 1.3 %collective-permute-start.1 = (bf16[8,256,128]{2,1,0:T(8,128)(2,1)S(1)}, bf16[8,256,128]{2,1,0:T(8,128)(2,1)S(1)}, u32[]{:S(2)}, u32[]{:S(2)}) collective-permute-start(bf16[8,256,128]{2,1,0:T(8,128)(2,1)S(1)} %all-to-all-done.1.own_ref), channel_id=1, source_target_pairs={{32,0},{36,4},{40,8},{44,12},{48,16},{52,20},{56,24},{60,28},{64,3... | collective-permute-start | bytes 1572872 | tf_op jit(solution)/shard_map/ppermute | solution.py:93
  51.5 5.5 %collective-permute-start = (bf16[8,256,128]{2,1,0:T(8,128)(2,1)S(1)}, bf16[8,256,128]{2,1,0:T(8,128)(2,1)S(1)}, u32[]{:S(2)}, u32[]{:S(2)}) collective-permute-start(bf16[8,256,128]{2,1,0:T(8,128)(2,1)S(1)} %all-to-all-done.1.own_ref), channel_id=1, source_target_pairs={{0,32},{4,36},{8,40},{12,44},{16,48},{20,52},{24,56},{28,60},{32,6... | collective-permute-start | bytes 1572872 | tf_op jit(solution)/shard_map/ppermute | solution.py:92
  57.1 0.2 select_reduce_fusion
  57.2 0.1 copy.9
  57.3 0.6 convert_element_type.21.flag_ref
  57.9 15.8 %collective-permute-done.2.opp_ref = bf16[8,256,128]{2,1,0:T(8,128)(2,1)S(1)} collective-permute-done((bf16[8,256,128]{2,1,0:T(8,128)(2,1)S(1)}, bf16[8,256,128]{2,1,0:T(8,128)(2,1)S(1)}, u32[]{:S(2)}, u32[]{:S(2)}) %collective-permute-start.2) | collective-permute-done | bytes 524320 | tf_op jit(solution)/shard_map/ppermute | solution.py:94
  73.6 20.3 %collective-permute-done.1.next_ref = bf16[8,256,128]{2,1,0:T(8,128)(2,1)S(1)} collective-permute-done((bf16[8,256,128]{2,1,0:T(8,128)(2,1)S(1)}, bf16[8,256,128]{2,1,0:T(8,128)(2,1)S(1)}, u32[]{:S(2)}, u32[]{:S(2)}) %collective-permute-start.1) | collective-permute-done | bytes 524320 | tf_op jit(solution)/shard_map/ppermute | solution.py:93
  94.0 0.8 copy-done.4
  94.8 0.8 copy-done.5
  95.6 5.6 %attend.1 = bf16[8,128,128]{2,1,0:T(8,128)(2,1)} custom-call(s32[8,10]{1,0:T(8,128)} %convert_element_type.21.flag_ref, bf16[8,144,128]{2,1,0:T(8,128)(2,1)} %copy-done.1, bf16[8,256,128]{2,1,0:T(8,128)(2,1)} %copy-done, bf16[8,256,128]{2,1,0:T(8,128)(2,1)} %copy-done.5, bf16[8,256,128]{2,1,0:T(8,128)(2,1)} %copy-done.4, bf16[8,256,128]{2,1,0:T(8,128)(2,1)} %copy-done.3), custom_call_target="tpu_custom_call" | custom-call | tf_op jit(solution)/shard_map/attend/pallas_call | solution.py:103
  101.2 18.9 %all_to_all.15 = bf16[8,128,128]{2,1,0:T(8,128)(2,1)S(1)} all-to-all(bf16[8,128,128]{2,1,0:T(8,128)(2,1)} %attend.1), channel_id=1, replica_groups={{0,4,8,12,16,20,24,28},{32,36,40,44,48,52,56,60},{64,68,72,76,80,84,88,..., dimensions={0} | all-to-all | bytes 524288 | tf_op jit(solution)/shard_map/all_to_all | solution.py:110
  120.1 0.2 copy.10
  120.3 0.9 copy.11
  (20 shorter events, 0.1 us)
Async XLA Ops:
  0.0 1.8 %copy-start.2 = (bf16[128,1024]{1,0:T(8,128)(2,1)S(1)}, bf16[128,1024]{1,0:T(8,128)(2,1)}, u32[]{:S(2)}) copy-start(bf16[128,1024]{1,0:T(8,128)(2,1)} %k_ref.1) | copy-start | bytes 786436
  17.8 18.0 %all-to-all-start.1 = ((bf16[8,256,128]{2,1,0:T(8,128)(2,1)}), bf16[8,256,128]{2,1,0:T(8,128)(2,1)S(1)}, u32[]{:S(2)}, u32[]{:S(2)}) async-start(bf16[8,256,128]{2,1,0:T(8,128)(2,1)} %get-tuple-element.8), calls=%async_computation.1 | async-start | bytes 1048576 | tf_op jit(solution)/shard_map/all_to_all | solution.py:87
  35.8 58.2 %copy-start = (bf16[8,256,128]{2,1,0:T(8,128)(2,1)}, bf16[8,256,128]{2,1,0:T(8,128)(2,1)S(1)}, u32[]{:S(2)}) copy-start(bf16[8,256,128]{2,1,0:T(8,128)(2,1)S(1)} %all-to-all-done.1.own_ref) | copy-start | bytes 1572868
  35.8 21.3 %all-to-all-start = ((bf16[8,144,128]{2,1,0:T(8,128)(2,1)}), bf16[8,144,128]{2,1,0:T(8,128)(2,1)S(1)}, u32[]{:S(2)}, u32[]{:S(2)}) async-start(bf16[8,144,128]{2,1,0:T(8,128)(2,1)} %get-tuple-element.7), calls=%async_computation | async-start | bytes 589824 | tf_op jit(solution)/shard_map/all_to_all | solution.py:95
  39.2 34.4 %collective-permute-start.2 = (bf16[8,256,128]{2,1,0:T(8,128)(2,1)S(1)}, bf16[8,256,128]{2,1,0:T(8,128)(2,1)S(1)}, u32[]{:S(2)}, u32[]{:S(2)}) collective-permute-start(bf16[8,256,128]{2,1,0:T(8,128)(2,1)S(1)} %all-to-all-done.1.own_ref), channel_id=1, source_target_pairs={{0,64},{4,68},{8,72},{12,76},{16,80},{20,84},{24,88},{28,92},{32,9... | collective-permute-start | bytes 1572872 | tf_op jit(solution)/shard_map/ppermute | solution.py:94
  50.2 43.8 %collective-permute-start.1 = (bf16[8,256,128]{2,1,0:T(8,128)(2,1)S(1)}, bf16[8,256,128]{2,1,0:T(8,128)(2,1)S(1)}, u32[]{:S(2)}, u32[]{:S(2)}) collective-permute-start(bf16[8,256,128]{2,1,0:T(8,128)(2,1)S(1)} %all-to-all-done.1.own_ref), channel_id=1, source_target_pairs={{32,0},{36,4},{40,8},{44,12},{48,16},{52,20},{56,24},{60,28},{64,3... | collective-permute-start | bytes 1572872 | tf_op jit(solution)/shard_map/ppermute | solution.py:93
  51.5 42.5 %collective-permute-start = (bf16[8,256,128]{2,1,0:T(8,128)(2,1)S(1)}, bf16[8,256,128]{2,1,0:T(8,128)(2,1)S(1)}, u32[]{:S(2)}, u32[]{:S(2)}) collective-permute-start(bf16[8,256,128]{2,1,0:T(8,128)(2,1)S(1)} %all-to-all-done.1.own_ref), channel_id=1, source_target_pairs={{0,32},{4,36},{8,40},{12,44},{16,48},{20,52},{24,56},{28,60},{32,6... | collective-permute-start | bytes 1572872 | tf_op jit(solution)/shard_map/ppermute | solution.py:92
  57.0 37.0 %copy-start.1 = (bf16[8,144,128]{2,1,0:T(8,128)(2,1)}, bf16[8,144,128]{2,1,0:T(8,128)(2,1)S(1)}, u32[]{:S(2)}) copy-start(bf16[8,144,128]{2,1,0:T(8,128)(2,1)S(1)} %all-to-all-done.qm_ref) | copy-start | bytes 884740
  73.6 20.4 %copy-start.3 = (bf16[8,256,128]{2,1,0:T(8,128)(2,1)}, bf16[8,256,128]{2,1,0:T(8,128)(2,1)S(1)}, u32[]{:S(2)}) copy-start(bf16[8,256,128]{2,1,0:T(8,128)(2,1)S(1)} %collective-permute-done.2.opp_ref) | copy-start | bytes 1572868
  94.0 0.8 copy-start.4
  94.8 0.8 copy-start.5

commit v2 on v1

v2 whole, which is shorter than its diff:
```python
import jax
import jax.numpy as jnp
from jax import lax
from jax.experimental import pallas as pl
from jax.experimental.pallas import tpu as pltpu
from jax.sharding import PartitionSpec as P


HEADS = 32
HD = 128
BLOCK = 128
ROW = 8
EXTRA = 16

epsilon = 1e-06
floor_score = -1e30
OFFSETS = (0, 1, -1, 2, -2, 4, -4, 8, -8)
FAR = len(OFFSETS)


def prep_kernel(q_ref, k_ref, tot_ref, qg_ref, kg_ref, mask_ref, k_out, qm_out):
    totals = jnp.concatenate([tot_ref[...], jnp.zeros((6, BLOCK), jnp.float32)], axis=0)
    factor = lax.rsqrt(totals / (HEADS * HD) + epsilon)
    columns = jnp.transpose(factor)
    qf, kf = columns[:, 0:1], columns[:, 1:2]
    blocks = mask_ref.shape[1]
    row = jnp.broadcast_to(mask_ref[...].astype(jnp.float32), (EXTRA, blocks)).astype(jnp.bfloat16)
    for h in range(ROW):
        cut = slice(h * HD, (h + 1) * HD)
        k = k_ref[:, cut].astype(jnp.float32) * kf * kg_ref[:, cut]
        k_out[h] = k.astype(jnp.bfloat16)
        q = q_ref[:, cut].astype(jnp.float32) * qf * qg_ref[:, cut]
        qm_out[h, :BLOCK, :] = q.astype(jnp.bfloat16)
        qm_out[h, BLOCK:, :] = jnp.zeros((EXTRA, HD), jnp.bfloat16)
        qm_out[h, BLOCK:, :blocks] = row


def near_kernel(flag_ref, qm_ref, k_own, k_prev, k_next, v_own, v_prev, v_next, acc_ref, stat_ref):
    key_rows = (k_prev, k_own, k_next)
    value_rows = (v_prev, v_own, v_next)
    for i in range(ROW):
        spots = [((ROW + i + d) // ROW, (ROW + i + d) % ROW) for d in OFFSETS]
        q = qm_ref[i, :BLOCK, :]
        keys = jnp.concatenate([key_rows[r][j] for r, j in spots], axis=0)
        scores = lax.dot_general(
            q, keys, (((1,), (1,)), ((), ())), preferred_element_type=jnp.float32
        ) * (HD ** (-0.5))
        parts = [
            jnp.where(flag_ref[i, n] > 0, scores[:, n * BLOCK : (n + 1) * BLOCK], floor_score)
            for n in range(len(spots))
        ]
        top = parts[0]
        for part in parts[1:]:
            top = jnp.maximum(top, part)
        row_max = jnp.max(top, axis=1, keepdims=True)
        weights = [jnp.exp(part - row_max) for part in parts]
        total = weights[0]
        for w in weights[1:]:
            total = total + w
        weight_sum = jnp.sum(total, axis=1, keepdims=True)
        rounded = jnp.concatenate([w.astype(jnp.bfloat16) for w in weights], axis=1)
        vals = jnp.concatenate([value_rows[r][j] for r, j in spots], axis=0)
        acc_ref[i] = jnp.dot(rounded, vals, preferred_element_type=jnp.float32)
        half = (BLOCK, HD // 2)
        stat_ref[i] = jnp.concatenate(
            [jnp.broadcast_to(row_max, half), jnp.broadcast_to(weight_sum, half)], axis=1
        )


def far_kernel(flag_ref, qm_ref, k_far, v_far, acc_ref, stat_ref, out_ref):
    each = range(ROW)
    scores = [
        lax.dot_general(
            qm_ref[i, :BLOCK, :],
            k_far[i],
            (((1,), (1,)), ((), ())),
            preferred_element_type=jnp.float32,
        )
        * (HD ** (-0.5))
        for i in each
    ]
    scores = [jnp.where(flag_ref[i, FAR] > 0, scores[i], floor_score) for i in each]
    old_max = [stat_ref[i, :, 0:1] for i in each]
    tops = [jnp.max(scores[i], axis=1, keepdims=True) for i in each]
    new_max = [jnp.maximum(old_max[i], tops[i]) for i in each]
    weights = [jnp.exp(scores[i] - new_max[i]) for i in each]
    extra = [
        jnp.dot(weights[i].astype(jnp.bfloat16), v_far[i], preferred_element_type=jnp.float32)
        for i in each
    ]
    sums = [jnp.sum(weights[i], axis=1, keepdims=True) for i in each]
    shrink = [jnp.exp(old_max[i] - new_max[i]) for i in each]
    for i in each:
        total = stat_ref[i, :, HD // 2 : HD // 2 + 1] * shrink[i] + sums[i]
        numer = acc_ref[i] * shrink[i] + extra[i]
        out_ref[i] = (numer / total).astype(jnp.bfloat16)


def local(queries, keys, values, query_gain, key_gain, block_mask):
    tokens = queries.shape[0]
    blocks = block_mask.shape[1]
    rows = blocks // ROW
    groups = [[z * ROW + y for y in range(ROW)] for z in range(rows)]
    z = lax.axis_index("ctx") // ROW
    tile = jax.ShapeDtypeStruct((ROW, BLOCK, HD), jnp.bfloat16)
    wide = jax.ShapeDtypeStruct((ROW, BLOCK, HD), jnp.float32)

    def spread(x):
        return lax.all_to_all(x, "ctx", 0, 0, axis_index_groups=groups)

    def shift(x, step):
        pairs = [(c, (c + step * ROW) % blocks) for c in range(blocks)]
        return lax.ppermute(x, "ctx", pairs)

    v = jnp.transpose(values.reshape(tokens, ROW, HD), (1, 0, 2))
    v = spread(v)

    sums = jnp.stack(
        [jnp.sum(jnp.square(a.astype(jnp.float32)), axis=1) for a in (queries, keys)]
    )
    totals = lax.psum(sums, "tp")
    k, qm = pl.pallas_call(
        prep_kernel,
        out_shape=(tile, jax.ShapeDtypeStruct((ROW, BLOCK + EXTRA, HD), jnp.bfloat16)),
        name="prep",
    )(queries, keys, totals, query_gain[None], key_gain[None], block_mask)
    k = spread(k)

    v_prev = shift(v, 1)
    v_next = shift(v, -1)
    k_prev = shift(k, 1)
    k_next = shift(k, -1)
    qm = spread(qm)
    v_far = shift(v_prev, 1)
    k_far = shift(k_next, -1)

    centre = z * ROW + jnp.arange(ROW)
    wanted = jnp.stack([centre + d for d in OFFSETS] + [centre ^ 16], axis=1)
    mask_rows = qm[:, BLOCK, :blocks].astype(jnp.float32)
    picked = wanted[:, :, None] == jnp.arange(blocks)[None, None, :]
    flags = jnp.sum(jnp.where(picked, mask_rows[:, None, :], 0.0), axis=2).astype(jnp.int32)

    smem, vmem = pl.BlockSpec(memory_space=pltpu.SMEM), pl.BlockSpec(memory_space=pltpu.VMEM)
    cost = pl.CostEstimate(flops=600_000_000, bytes_accessed=4_000_000, transcendentals=1_200_000)
    acc, stat = pl.pallas_call(
        near_kernel,
        out_shape=(wide, wide),
        in_specs=[smem] + [vmem] * 7,
        cost_estimate=cost,
        name="near",
    )(flags, qm, k, k_prev, k_next, v, v_prev, v_next)
    out = pl.pallas_call(
        far_kernel,
        out_shape=tile,
        in_specs=[smem] + [vmem] * 5,
        name="far",
    )(flags, qm, k_far, v_far, acc, stat)
    out = spread(out)
    return jnp.transpose(out, (1, 0, 2)).reshape(queries.shape)


def solution(mesh):
    in_specs = (
        P(("dp", "ctx"), "tp"),
        P(("dp", "ctx"), "tp"),
        P(("dp", "ctx"), "tp"),
        P("tp"),
        P("tp"),
        P("ctx", None),
    )
    out_specs = P(("dp", "ctx"), "tp")

    return jax.shard_map(local, mesh=mesh, in_specs=in_specs, out_specs=out_specs, check_vma=False)
```

time: 123 us -> 121 us (0.984)
  the two profiles are of different devices: /device:TPU:6 before, /device:TPU:64 now
where the time goes in v2:
time: 121 us; the launch traced here: 120 us
  starting transfers between devices  40.7 us (34%)
  waiting for transfers between devices  33 us (27%)
  blocking collectives  28.4 us (23%)
  Pallas kernels  11.7 us (10%)
  local copies, waits for them, and re-layouts  4.33 us (4%)
  other arithmetic  2.05 us (2%)
    ppermute x6, starting transfers between devices, shift(): return lax.ppermute(x, 'ctx', pairs)  26.6 us
    all_to_all x3, waiting for transfers between devices, spread(): return lax.all_to_all(x, 'ctx', 0, 0, axis_index_groups=groups)  19.8 us
    all_to_all x1, blocking collectives, spread(): return lax.all_to_all(x, 'ctx', 0, 0, axis_index_groups=groups)  17.3 us
    all_to_all x3, starting transfers between devices, spread(): return lax.all_to_all(x, 'ctx', 0, 0, axis_index_groups=groups)  14.1 us
    ppermute x6, waiting for transfers between devices, shift(): return lax.ppermute(x, 'ctx', pairs)  13.1 us
    psum x1, blocking collectives, local(): totals = lax.psum(sums, 'tp')  11.1 us
    pallas_call x1, Pallas kernels, local(): pl.pallas_call(near_kernel, out_shape=(wide, wide), in_specs=[smem] + [vm...  5.6 us
    pallas_call x1, Pallas kernels, local(): pl.pallas_call(far_kernel, out_shape=tile, in_specs=[smem] + [vmem] * 5,...  3.99 us
  transfers between devices with their start and end apart: 9, of which 4 were waited for; matrix products, arithmetic and copies ran while one was open for 2% of the time, Pallas kernels for 5%

profile of v2, /device:TPU:64, one launch (start us, length us, event | category | flops | bytes accessed | tf_op | source)
XLA Modules:
  0.0 120.4 jit_solution(12147617624811113624)
XLA Ops:
  0.0 1.1 multiply_reduce_fusion.1
  1.3 11.1 %psum.7.tot_ref = f32[2,128]{1,0:T(2,128)} all-reduce(f32[2,128]{1,0:T(2,128)S(1)} %pad_maximum_fusion), channel_id=1, replica_groups=mesh['dp'=4,'ctx'=32,'tp'=4] {'tp'}, use_global_device_ids=true, to_apply=%region_2.3 | all-reduce | flops 256 | bytes 2048 | tf_op jit(solution)/shard_map/psum | solution.py:121
  12.3 2.1 %prep.1 = (bf16[8,128,128]{2,1,0:T(8,128)(2,1)}, bf16[8,144,128]{2,1,0:T(8,128)(2,1)}) custom-call(bf16[128,1024]{1,0:T(8,128)(2,1)} %q_ref.1, bf16[128,1024]{1,0:T(8,128)(2,1)} %k_ref.1, f32[2,128]{1,0:T(2,128)} %psum.7.tot_ref, f32[1,1024]{1,0:T(1,128)} %bitcast.13, f32[1,1024]{1,0:T(1,128)} %bitcast.14, s32[1,32]{1,0:T(1,128)} %mask_ref.1), custom_call_target="tpu_custom_call" | custom-call | tf_op jit(solution)/shard_map/prep/pallas_call | solution.py:122
  14.4 7.2 %all-to-all-start.1 = ((bf16[8,128,128]{2,1,0:T(8,128)(2,1)}), bf16[8,128,128]{2,1,0:T(8,128)(2,1)S(1)}, u32[]{:S(2)}, u32[]{:S(2)}) async-start(bf16[8,128,128]{2,1,0:T(8,128)(2,1)} %get-tuple-element.10), calls=%async_computation.1 | async-start | bytes 524288 | tf_op jit(solution)/shard_map/all_to_all | solution.py:109
  21.9 0.8 copy.13
  22.7 9.5 %all-to-all-done.1.k_own = bf16[8,128,128]{2,1,0:T(8,128)(2,1)S(1)} async-done(((bf16[8,128,128]{2,1,0:T(8,128)(2,1)}), bf16[8,128,128]{2,1,0:T(8,128)(2,1)S(1)}, u32[]{:S(2)}, u32[]{:S(2)}) %all-to-all-start.1) | async-done | bytes 262176 | tf_op jit(solution)/shard_map/all_to_all | solution.py:109
  32.2 3.4 %all-to-all-start.2 = ((bf16[8,128,128]{2,1,0:T(8,128)(2,1)}), bf16[8,128,128]{2,1,0:T(8,128)(2,1)S(1)}, u32[]{:S(2)}, u32[]{:S(2)}) async-start(bf16[8,128,128]{2,1,0:T(8,128)(2,1)} %bitcast.6), calls=%async_computation.2 | async-start | bytes 524288 | tf_op jit(solution)/shard_map/all_to_all | solution.py:109
  35.6 10.4 %all-to-all-done.2.v_own = bf16[8,128,128]{2,1,0:T(8,128)(2,1)S(1)} async-done(((bf16[8,128,128]{2,1,0:T(8,128)(2,1)}), bf16[8,128,128]{2,1,0:T(8,128)(2,1)S(1)}, u32[]{:S(2)}, u32[]{:S(2)}) %all-to-all-start.2) | async-done | bytes 262176 | tf_op jit(solution)/shard_map/all_to_all | solution.py:109
  46.0 3.4 %all-to-all-start = ((bf16[8,144,128]{2,1,0:T(8,128)(2,1)}), bf16[8,144,128]{2,1,0:T(8,128)(2,1)S(1)}, u32[]{:S(2)}, u32[]{:S(2)}) async-start(bf16[8,144,128]{2,1,0:T(8,128)(2,1)} %get-tuple-element.9), calls=%async_computation | async-start | bytes 589824 | tf_op jit(solution)/shard_map/all_to_all | solution.py:109
  49.4 10.0 %collective-permute-start = (bf16[8,128,128]{2,1,0:T(8,128)(2,1)S(1)}, bf16[8,128,128]{2,1,0:T(8,128)(2,1)S(1)}, u32[]{:S(2)}, u32[]{:S(2)}) collective-permute-start(bf16[8,128,128]{2,1,0:T(8,128)(2,1)S(1)} %all-to-all-done.1.k_own), channel_id=1, source_target_pairs={{0,96},{4,100},{8,104},{12,108},{16,112},{20,116},{24,120},{28,124... | collective-permute-start | bytes 786440 | tf_op jit(solution)/shard_map/ppermute | solution.py:113
  59.5 1.9 %collective-permute-start.2 = (bf16[8,128,128]{2,1,0:T(8,128)(2,1)S(1)}, bf16[8,128,128]{2,1,0:T(8,128)(2,1)S(1)}, u32[]{:S(2)}, u32[]{:S(2)}) collective-permute-start(bf16[8,128,128]{2,1,0:T(8,128)(2,1)S(1)} %all-to-all-done.2.v_own), channel_id=1, source_target_pairs={{0,32},{4,36},{8,40},{12,44},{16,48},{20,52},{24,56},{28,60},{32,6... | collective-permute-start | bytes 786440 | tf_op jit(solution)/shard_map/ppermute | solution.py:113
  61.5 2.4 %collective-permute-start.4 = (bf16[8,128,128]{2,1,0:T(8,128)(2,1)S(1)}, bf16[8,128,128]{2,1,0:T(8,128)(2,1)S(1)}, u32[]{:S(2)}, u32[]{:S(2)}) collective-permute-start(bf16[8,128,128]{2,1,0:T(8,128)(2,1)S(1)} %all-to-all-done.1.k_own), channel_id=1, source_target_pairs={{0,32},{4,36},{8,40},{12,44},{16,48},{20,52},{24,56},{28,60},{32,6... | collective-permute-start | bytes 786440 | tf_op jit(solution)/shard_map/ppermute | solution.py:113
  64.0 5.5 %collective-permute-start.5 = (bf16[8,128,128]{2,1,0:T(8,128)(2,1)S(1)}, bf16[8,128,128]{2,1,0:T(8,128)(2,1)S(1)}, u32[]{:S(2)}, u32[]{:S(2)}) collective-permute-start(bf16[8,128,128]{2,1,0:T(8,128)(2,1)S(1)} %all-to-all-done.2.v_own), channel_id=1, source_target_pairs={{0,96},{4,100},{8,104},{12,108},{16,112},{20,116},{24,120},{28,124... | collective-permute-start | bytes 786440 | tf_op jit(solution)/shard_map/ppermute | solution.py:113
  69.5 4.8 %collective-permute-start.1 = (bf16[8,128,128]{2,1,0:T(8,128)(2,1)S(1)}, bf16[8,128,128]{2,1,0:T(8,128)(2,1)S(1)}, u32[]{:S(2)}, u32[]{:S(2)}) collective-permute-start(bf16[8,128,128]{2,1,0:T(8,128)(2,1)S(1)} %collective-permute-done.k_next), channel_id=1, source_target_pairs={{0,96},{4,100},{8,104},{12,108},{16,112},{20,116},{24,120},{28,124... | collective-permute-start | bytes 786440 | tf_op jit(solution)/shard_map/ppermute | solution.py:113
  74.3 5.0 %collective-permute-done.2.v_prev = bf16[8,128,128]{2,1,0:T(8,128)(2,1)S(1)} collective-permute-done((bf16[8,128,128]{2,1,0:T(8,128)(2,1)S(1)}, bf16[8,128,128]{2,1,0:T(8,128)(2,1)S(1)}, u32[]{:S(2)}, u32[]{:S(2)}) %collective-permute-start.2) | collective-permute-done | bytes 262176 | tf_op jit(solution)/shard_map/ppermute | solution.py:113
  79.3 1.9 %collective-permute-start.3 = (bf16[8,128,128]{2,1,0:T(8,128)(2,1)S(1)}, bf16[8,128,128]{2,1,0:T(8,128)(2,1)S(1)}, u32[]{:S(2)}, u32[]{:S(2)}) collective-permute-start(bf16[8,128,128]{2,1,0:T(8,128)(2,1)S(1)} %collective-permute-done.2.v_prev), channel_id=1, source_target_pairs={{0,32},{4,36},{8,40},{12,44},{16,48},{20,52},{24,56},{28,60},{32,6... | collective-permute-start | bytes 786440 | tf_op jit(solution)/shard_map/ppermute | solution.py:113
  82.0 8.2 %collective-permute-done.4.k_prev = bf16[8,128,128]{2,1,0:T(8,128)(2,1)S(1)} collective-permute-done((bf16[8,128,128]{2,1,0:T(8,128)(2,1)S(1)}, bf16[8,128,128]{2,1,0:T(8,128)(2,1)S(1)}, u32[]{:S(2)}, u32[]{:S(2)}) %collective-permute-start.4) | collective-permute-done | bytes 262176 | tf_op jit(solution)/shard_map/ppermute | solution.py:113
  90.3 0.7 copy-done.9
  90.9 0.7 copy-done.10
  91.6 5.6 %near.1 = (f32[8,128,128]{2,1,0:T(8,128)}, f32[8,128,128]{2,1,0:T(8,128)}) custom-call(s32[8,10]{1,0:T(8,128)} %convert_element_type.13.flag_ref, bf16[8,144,128]{2,1,0:T(8,128)(2,1)} %copy-done, bf16[8,128,128]{2,1,0:T(8,128)(2,1)} %copy-done.3, bf16[8,128,128]{2,1,0:T(8,128)(2,1)} %copy-done.9, bf16[8,128,128]{2,1,0:T(8,128)(2,1)} %copy-done.7, ...), custom_call_target="tpu_custom_call" | custom-call | flops 600000000 | bytes 4000000 | tf_op jit(solution)/shard_map/near/pallas_call | solution.py:145
  97.3 0.7 copy-done.5
  98.0 4.0 %far.1 = bf16[8,128,128]{2,1,0:T(8,128)(2,1)} custom-call(s32[8,10]{1,0:T(8,128)} %convert_element_type.13.flag_ref, bf16[8,144,128]{2,1,0:T(8,128)(2,1)} %copy-done, bf16[8,128,128]{2,1,0:T(8,128)(2,1)} %copy-done.5, bf16[8,128,128]{2,1,0:T(8,128)(2,1)} %copy-done.6, f32[8,128,128]{2,1,0:T(8,128)} %get-tuple-element.11.acc_ref, ...), custom_call_target="tpu_custom_call" | custom-call | tf_op jit(solution)/shard_map/far/pallas_call | solution.py:152
  102.0 17.3 %all_to_all.20 = bf16[8,128,128]{2,1,0:T(8,128)(2,1)S(1)} all-to-all(bf16[8,128,128]{2,1,0:T(8,128)(2,1)} %far.1), channel_id=1, replica_groups={{0,4,8,12,16,20,24,28},{32,36,40,44,48,52,56,60},{64,68,72,76,80,84,88,..., dimensions={0} | all-to-all | bytes 524288 | tf_op jit(solution)/shard_map/all_to_all | solution.py:109
  119.5 0.9 copy.15
  (38 shorter events, 1.5 us)
Async XLA Ops:
  0.0 1.1 copy-start.1
  14.4 7.2 %copy-start.2 = (bf16[128,1024]{1,0:T(8,128)(2,1)S(1)}, bf16[128,1024]{1,0:T(8,128)(2,1)}, u32[]{:S(2)}) copy-start(bf16[128,1024]{1,0:T(8,128)(2,1)} %param.8) | copy-start | bytes 786436
  14.4 17.7 %all-to-all-start.1 = ((bf16[8,128,128]{2,1,0:T(8,128)(2,1)}), bf16[8,128,128]{2,1,0:T(8,128)(2,1)S(1)}, u32[]{:S(2)}, u32[]{:S(2)}) async-start(bf16[8,128,128]{2,1,0:T(8,128)(2,1)} %get-tuple-element.10), calls=%async_computation.1 | async-start | bytes 524288 | tf_op jit(solution)/shard_map/all_to_all | solution.py:109
  32.2 29.3 %copy-start.3 = (bf16[8,128,128]{2,1,0:T(8,128)(2,1)}, bf16[8,128,128]{2,1,0:T(8,128)(2,1)S(1)}, u32[]{:S(2)}) copy-start(bf16[8,128,128]{2,1,0:T(8,128)(2,1)S(1)} %all-to-all-done.1.k_own) | copy-start | bytes 786436
  32.2 13.8 %all-to-all-start.2 = ((bf16[8,128,128]{2,1,0:T(8,128)(2,1)}), bf16[8,128,128]{2,1,0:T(8,128)(2,1)S(1)}, u32[]{:S(2)}, u32[]{:S(2)}) async-start(bf16[8,128,128]{2,1,0:T(8,128)(2,1)} %bitcast.6), calls=%async_computation.2 | async-start | bytes 524288 | tf_op jit(solution)/shard_map/all_to_all | solution.py:109
  46.0 18.0 %copy-start.4 = (bf16[8,128,128]{2,1,0:T(8,128)(2,1)}, bf16[8,128,128]{2,1,0:T(8,128)(2,1)S(1)}, u32[]{:S(2)}) copy-start(bf16[8,128,128]{2,1,0:T(8,128)(2,1)S(1)} %all-to-all-done.2.v_own) | copy-start | bytes 786436
  46.0 35.2 %all-to-all-start = ((bf16[8,144,128]{2,1,0:T(8,128)(2,1)}), bf16[8,144,128]{2,1,0:T(8,128)(2,1)S(1)}, u32[]{:S(2)}, u32[]{:S(2)}) async-start(bf16[8,144,128]{2,1,0:T(8,128)(2,1)} %get-tuple-element.9), calls=%async_computation | async-start | bytes 589824 | tf_op jit(solution)/shard_map/all_to_all | solution.py:109
  49.4 20.0 %collective-permute-start = (bf16[8,128,128]{2,1,0:T(8,128)(2,1)S(1)}, bf16[8,128,128]{2,1,0:T(8,128)(2,1)S(1)}, u32[]{:S(2)}, u32[]{:S(2)}) collective-permute-start(bf16[8,128,128]{2,1,0:T(8,128)(2,1)S(1)} %all-to-all-done.1.k_own), channel_id=1, source_target_pairs={{0,96},{4,100},{8,104},{12,108},{16,112},{20,116},{24,120},{28,124... | collective-permute-start | bytes 786440 | tf_op jit(solution)/shard_map/ppermute | solution.py:113
  59.5 19.8 %collective-permute-start.2 = (bf16[8,128,128]{2,1,0:T(8,128)(2,1)S(1)}, bf16[8,128,128]{2,1,0:T(8,128)(2,1)S(1)}, u32[]{:S(2)}, u32[]{:S(2)}) collective-permute-start(bf16[8,128,128]{2,1,0:T(8,128)(2,1)S(1)} %all-to-all-done.2.v_own), channel_id=1, source_target_pairs={{0,32},{4,36},{8,40},{12,44},{16,48},{20,52},{24,56},{28,60},{32,6... | collective-permute-start | bytes 786440 | tf_op jit(solution)/shard_map/ppermute | solution.py:113
  61.5 28.7 %collective-permute-start.4 = (bf16[8,128,128]{2,1,0:T(8,128)(2,1)S(1)}, bf16[8,128,128]{2,1,0:T(8,128)(2,1)S(1)}, u32[]{:S(2)}, u32[]{:S(2)}) collective-permute-start(bf16[8,128,128]{2,1,0:T(8,128)(2,1)S(1)} %all-to-all-done.1.k_own), channel_id=1, source_target_pairs={{0,32},{4,36},{8,40},{12,44},{16,48},{20,52},{24,56},{28,60},{32,6... | collective-permute-start | bytes 786440 | tf_op jit(solution)/shard_map/ppermute | solution.py:113
  64.0 26.3 %collective-permute-start.5 = (bf16[8,128,128]{2,1,0:T(8,128)(2,1)S(1)}, bf16[8,128,128]{2,1,0:T(8,128)(2,1)S(1)}, u32[]{:S(2)}, u32[]{:S(2)}) collective-permute-start(bf16[8,128,128]{2,1,0:T(8,128)(2,1)S(1)} %all-to-all-done.2.v_own), channel_id=1, source_target_pairs={{0,96},{4,100},{8,104},{12,108},{16,112},{20,116},{24,120},{28,124... | collective-permute-start | bytes 786440 | tf_op jit(solution)/shard_map/ppermute | solution.py:113
  69.5 20.8 %copy-start.7 = (bf16[8,128,128]{2,1,0:T(8,128)(2,1)}, bf16[8,128,128]{2,1,0:T(8,128)(2,1)S(1)}, u32[]{:S(2)}) copy-start(bf16[8,128,128]{2,1,0:T(8,128)(2,1)S(1)} %collective-permute-done.k_next) | copy-start | bytes 786436
  69.5 27.7 %collective-permute-start.1 = (bf16[8,128,128]{2,1,0:T(8,128)(2,1)S(1)}, bf16[8,128,128]{2,1,0:T(8,128)(2,1)S(1)}, u32[]{:S(2)}, u32[]{:S(2)}) collective-permute-start(bf16[8,128,128]{2,1,0:T(8,128)(2,1)S(1)} %collective-permute-done.k_next), channel_id=1, source_target_pairs={{0,96},{4,100},{8,104},{12,108},{16,112},{20,116},{24,120},{28,124... | collective-permute-start | bytes 786440 | tf_op jit(solution)/shard_map/ppermute | solution.py:113
  79.3 11.0 %copy-start.8 = (bf16[8,128,128]{2,1,0:T(8,128)(2,1)}, bf16[8,128,128]{2,1,0:T(8,128)(2,1)S(1)}, u32[]{:S(2)}) copy-start(bf16[8,128,128]{2,1,0:T(8,128)(2,1)S(1)} %collective-permute-done.2.v_prev) | copy-start | bytes 786436
  79.3 18.0 %collective-permute-start.3 = (bf16[8,128,128]{2,1,0:T(8,128)(2,1)S(1)}, bf16[8,128,128]{2,1,0:T(8,128)(2,1)S(1)}, u32[]{:S(2)}, u32[]{:S(2)}) collective-permute-start(bf16[8,128,128]{2,1,0:T(8,128)(2,1)S(1)} %collective-permute-done.2.v_prev), channel_id=1, source_target_pairs={{0,32},{4,36},{8,40},{12,44},{16,48},{20,52},{24,56},{28,60},{32,6... | collective-permute-start | bytes 786440 | tf_op jit(solution)/shard_map/ppermute | solution.py:113
  81.2 9.1 %copy-start = (bf16[8,144,128]{2,1,0:T(8,128)(2,1)}, bf16[8,144,128]{2,1,0:T(8,128)(2,1)S(1)}, u32[]{:S(2)}) copy-start(bf16[8,144,128]{2,1,0:T(8,128)(2,1)S(1)} %all-to-all-done.qm_ref) | copy-start | bytes 884740
  90.2 0.7 copy-start.9
  90.9 0.7 copy-start.10
  97.2 0.7 copy-start.5
  97.2 0.8 copy-start.6
